TPU v7x, 512 devices: a whole 4x8x8 slice. The times are simulated.
512 devices in a mesh: dp: 128 (over y, z, core), term: 4 (over x).
Axes of the slice: x: 4, y: 8, z: 8, core: 2. Of those that a mesh axis runs over, the one named last changes fastest.
Arguments:
- hidden: bfloat16 [128, 256, 768], P('dp'), may hold values from -100 to 100, as said below
- segment_ids: int32 [128, 256], replicated, may hold values from 0 to 3, never falling along the last dimension, each value on 1 to 160 neighbouring positions
- block_lists: int32 [512, 128], replicated, may hold values from 0 to 255, all different within a row
- doc_ids: int32 [512], replicated, may hold values from 0 to 511, each once
- attn_gain: float32 [768], replicated, may hold values from 0.1 to 1.9
- qkv_weight: bfloat16 [3, 768, 768], P(None, None, 'term'), may hold values from -0.21875 to 0.21875
- attn_out: bfloat16 [768, 768], P('term'), may hold values from -0.21875 to 0.21875
- mlp_gain: float32 [768], replicated, may hold values from 0.1 to 1.9
- ffn_in: bfloat16 [2, 768, 1152], P(None, None, 'term'), may hold values from -0.21875 to 0.21875
- ffn_out: bfloat16 [1152, 768], P('term'), may hold values from -0.1875 to 0.1875
- final_gain: float32 [768], replicated, may hold values from 0.1 to 1.9
- head_dense: bfloat16 [768, 768], replicated, may hold values from -0.21875 to 0.21875
- head_gain: float32 [768], replicated, may hold values from 0.1 to 1.9
- decoder: bfloat16 [4, 8, 128, 8, 768], P('term', None, 'dp'), may hold values from -0.21875 to 0.21875
- decoder_bias: bfloat16 [4, 8, 128, 8], P('term', None, 'dp'), may hold values from -5 to 5
Outputs:
- postings: float32 [4, 8, 128, 8, 512], P('term', None, 'dp')
Inputs may be any that keep to these rules, and one draw needn't show every extreme that they name: `hidden`: every token has its own scale, and every feature its own scale. `segment_ids`: each row's numbers never fall and each of 0 to 3 appears; a passage has 1 to 160 tokens, and some passage of each row has exactly 160. `block_lists`: a passage lists 128 different blocks; every block is listed by some passage. `doc_ids`: each column appears once.
All inputs are finite; a program needn't handle non-finite values.
Results may differ from a plain program's by a relative error of at most 0.0035.
Values may be sent and summed in bfloat16 or wider, within the bound.
No kernel may reach another device: no remote copies, remote signals or barrier semaphores. Data moves between devices by JAX's collectives and lax.ppermute only.
A program may use at most 128 MiB of HBM per device.

v0:
```python
import jax
import jax.numpy as jnp
from jax import lax
from jax.sharding import PartitionSpec as P

BLOCK = 128
HALF_WIN = 64
PASS_DEV = 4
HEAD_DIM = 64


def layer_norm(values, gain_vec):
    average = jnp.mean(values, axis=-1, keepdims=True)
    centered = values - average
    spread = jnp.mean(centered * centered, axis=-1, keepdims=True)
    return centered * lax.rsqrt(spread + 1e-05) * gain_vec


def rotary(values, positions):
    half_dim = values.shape[-1] // 2
    frequency = 10000.0 ** (-2.0 * jnp.arange(half_dim, dtype=jnp.float32) / values.shape[-1])
    angles = positions.astype(jnp.float32)[:, None] * frequency[None, :]
    cosine = jnp.cos(angles)[:, None, :]
    sine_part = jnp.sin(angles)[:, None, :]
    first_half = values[..., :half_dim]
    second = values[..., half_dim:]
    return jnp.concatenate(
        [first_half * cosine - second * sine_part, second * cosine + first_half * sine_part],
        axis=-1,
    )


def head_block(residual, final_gain, head_dense, head_gain):
    normed_out = layer_norm(residual, final_gain).astype(jnp.bfloat16)
    dense_out = jnp.dot(normed_out, head_dense, preferred_element_type=jnp.float32)
    return layer_norm(jax.nn.gelu(dense_out, approximate=False), head_gain).astype(jnp.bfloat16)


def passage_maxima(activity, segments):
    return jnp.stack(
        [
            jnp.max(jnp.where(segments[..., None] == passage, activity, 0.0), axis=-2)
            for passage in range(PASS_DEV)
        ],
        axis=-2,
    )


def on_device(
    hidden,
    segment_ids,
    block_lists,
    doc_ids,
    attn_gain,
    qkv_weight,
    attn_out,
    mlp_gain,
    ffn_in,
    ffn_out,
    final_gain,
    head_dense,
    head_gain,
    decoder,
    decoder_bias,
):
    row_index = lax.axis_index("dp")
    dp_count = lax.axis_size("dp")
    tokens = hidden[0]
    length = tokens.shape[0]
    width = tokens.shape[1]
    segments = lax.dynamic_index_in_dim(segment_ids, row_index, 0, keepdims=False)
    token_index = jnp.arange(length, dtype=jnp.int32)
    positions = token_index - jnp.sum(
        (segments[None, :] < segments[:, None]).astype(jnp.int32), axis=1
    )
    allowed = (segments[:, None] == segments[None, :]) & (
        jnp.abs(token_index[:, None] - token_index[None, :]) <= HALF_WIN
    )
    normed = layer_norm(tokens.astype(jnp.float32), attn_gain).astype(jnp.bfloat16)
    head_width = qkv_weight.shape[2]
    local_heads = head_width // HEAD_DIM

    def project(which_slot):
        return jnp.dot(normed, qkv_weight[which_slot], preferred_element_type=jnp.float32).reshape(
            length, local_heads, HEAD_DIM
        )

    queries = rotary(project(0), positions).astype(jnp.bfloat16)
    key_rows = rotary(project(1), positions).astype(jnp.bfloat16)
    values = project(2).astype(jnp.bfloat16)
    scores = jnp.einsum(
        "qhd,khd->hqk", queries, key_rows, preferred_element_type=jnp.float32
    ) * HEAD_DIM ** (-0.5)
    raised = jnp.where(allowed[None], jnp.exp(scores), 0.0)
    probabilities = (raised / jnp.sum(raised, axis=-1, keepdims=True)).astype(jnp.bfloat16)
    context = jnp.einsum("hqk,khd->qhd", probabilities, values, preferred_element_type=jnp.float32)
    context = context.astype(jnp.bfloat16).reshape(length, head_width)
    partial_attn = jnp.dot(context, attn_out, preferred_element_type=jnp.float32)
    after_attn = tokens.astype(jnp.float32) + lax.psum(partial_attn, "term")
    mixed_in = layer_norm(after_attn, mlp_gain).astype(jnp.bfloat16)
    inner_up = jnp.dot(mixed_in, ffn_in[0], preferred_element_type=jnp.float32)
    gate_part = jnp.dot(mixed_in, ffn_in[1], preferred_element_type=jnp.float32)
    activated = (jax.nn.gelu(inner_up, approximate=False) * gate_part).astype(jnp.bfloat16)
    partial_ffn = jnp.dot(activated, ffn_out, preferred_element_type=jnp.float32)
    summed = lax.psum(partial_ffn, "term")
    headed = head_block(after_attn + summed, final_gain, head_dense, head_gain)
    groups = decoder.shape[1]
    span = decoder.shape[3]
    part_terms = dp_count * span
    range_width = groups * part_terms
    range_start = lax.axis_index("term") * range_width
    passages = block_lists.shape[0]
    rows_weight = lax.all_gather(decoder, "dp", axis=2, tiled=True)
    rows_bias = lax.all_gather(decoder_bias, "dp", axis=2, tiled=True)
    count = rows_weight.shape[2]
    flat_rows = rows_weight[0].reshape(groups * count * span, width)
    logits = lax.dot_general(
        headed, flat_rows, (((1,), (1,)), ((), ())), preferred_element_type=jnp.float32
    )
    logits = logits + rows_bias[0].reshape(groups * count * span).astype(jnp.float32)[None, :]
    activity = jnp.log1p(jnp.maximum(logits, 0.0))
    maxima = passage_maxima(activity, segments).reshape(PASS_DEV, groups, count, span)
    term_order = jnp.arange(range_width, dtype=jnp.int32)
    term_blocks = (range_start + term_order) // BLOCK
    own_lists = lax.dynamic_slice_in_dim(block_lists, row_index * PASS_DEV, PASS_DEV, 0)
    listed = jnp.any(own_lists[:, :, None] == term_blocks[None, None, :], axis=1).astype(
        jnp.float32
    )
    weighted = maxima * listed.reshape(PASS_DEV, groups, dp_count, span)
    received = lax.all_to_all(weighted, "dp", split_axis=2, concat_axis=0, tiled=True)
    own_weights = received[:, :, 0, :]
    placed = (
        jnp.zeros((groups, span, passages), jnp.float32)
        .at[:, :, doc_ids]
        .set(jnp.transpose(own_weights, (1, 2, 0)))
    )
    return placed[None, :, None]


def solution(mesh):
    in_specs = (
        P("dp", None, None),
        P(),
        P(),
        P(),
        P(),
        P(None, None, "term"),
        P("term", None),
        P(),
        P(None, None, "term"),
        P("term", None),
        P(),
        P(),
        P(),
        P("term", None, "dp", None, None),
        P("term", None, "dp", None),
    )
    out_specs = P("term", None, "dp", None, None)
    return jax.shard_map(
        on_device, mesh=mesh, in_specs=in_specs, out_specs=out_specs, check_vma=False
    )
```

profile of v0, /device:TPU:1, one launch (start us, length us, event | category | flops | bytes accessed | tf_op | source)
XLA Modules:
  0.0 268.6 jit_solution(5582998730450174788)
XLA Ops:
  7.4 0.8 constant_dynamic-slice_fusion
  8.2 0.1 convert_reduce_fusion.1
  8.3 0.1 fusion.97
  8.5 1.1 convert_reduce_fusion
  9.6 1.2 fusion.9
  10.9 1.2 fusion.182
  12.1 0.2 fusion.30
  12.3 0.3 fusion.184
  12.6 0.3 fusion.185
  12.9 0.2 multiply_cosine_fusion
  13.2 1.2 fusion.3
  14.4 1.8 convolution_convert_fusion
  16.2 1.2 fusion.186
  17.5 58.9 %all-reduce.3.cloned.1.call-done = f32[256,768]{1,0:T(8,128)} async-done(((f32[256,768]{1,0:T(8,128)}), f32[256,768]{1,0:T(8,128)}) %all-reduce.3.cloned.1.call-update) | async-done | bytes 786448 | tf_op jit(solution)/shard_map/psum | solution.py:99
  76.4 1.4 fusion.140
  77.8 1.4 multiply_reduce_fusion.2
  79.2 0.2 multiply_convert_fusion.2
  79.4 1.3 fusion.24
  80.7 3.3 %fusion.5 = f32[256,768]{1,0:T(8,128)} fusion(bf16[288,768]{1,0:T(8,128)(2,1)S(1)} %copy-done.8, bf16[256,768]{1,0:T(8,128)(2,1)S(1)} %multiply_convert_fusion.2, bf16[2,768,288]{1,2,0:T(8,128)(2,1)} %param.23, f32[256,288]{0,1:T(8,128)S(1)} %fusion.24), kind=kOutput, calls=%fused_computation.19 | convolution fusion | flops 231358464 | bytes 2359296 | tf_op jit(solution)/shard_map/dot_general | solution.py:104
  84.1 0.5 all-gather.2.cloned.1.call-update
  84.6 53.9 %all_gather.7 = bf16[1,8,128,8]{3,1,0,2:T(8,128)(2,1)S(1)} all-gather(bf16[1,8,1,8]{3,1,0,2:T(8,128)(2,1)S(1)} %bitcast.86), channel_id=1, replica_groups=mesh['dp'=128,'term'=4] {'dp'}, dimensions={2}, use_global_device_ids=true | all-gather | bytes 16512 | tf_op jit(solution)/shard_map/all_gather | solution.py:114
  138.5 0.2 copy.42
  138.7 0.1 copy.43
  138.9 0.3 reshape.297
  139.1 0.7 constant_dynamic-slice_fusion.1
  139.9 2.6 compare_reduce_fusion
  142.5 1.3 reduce_or.12
  143.8 1.3 fusion.180
  145.1 0.2 multiply_reduce_fusion.1
  145.4 2.1 fusion.183
  147.6 0.2 multiply_reduce_fusion
  147.8 36.3 %all-gather.2.cloned.1.call-done = bf16[1,8,128,8,768]{4,3,2,1,0:T(8,128)(2,1)} async-done(((bf16[1,8,1,8,768]{4,3,2,1,0:T(8,128)(2,1)}), bf16[1,8,128,8,768]{4,3,2,1,0:T(8,128)(2,1)}) %all-gather.2.cloned.1.call-update) | async-done | bytes 12582928 | tf_op jit(solution)/shard_map/all_gather | solution.py:113
  184.2 10.7 %select_reduce_fusion.3 = (f32[8192]{0:T(1024)S(1)}, f32[8192]{0:T(1024)S(1)}, f32[8192]{0:T(1024)S(1)}, f32[8192]{0:T(1024)S(1)}) fusion(pred[256]{0:T(512)(128)(4,1)S(1)} %get-tuple-element.25, pred[256]{0:T(512)(128)(4,1)S(1)} %get-tuple-element.23, pred[256]{0:T(512)(128)(4,1)S(1)} %get-tuple-element.24, pred[256]{0:T(512)(128)(4,1)S(1)} %get-tuple-element.22, ...), kind=kOutput, calls=%fused_computation.8 | convolution fusion | flops 3242950656 | bytes 13539328 | tf_op jit(solution)/shard_map/dot_general | solution.py:117
  194.9 0.3 stack.15
  195.2 0.3 stack.16
  195.5 0.3 stack.17
  195.8 1.1 stack.18
  196.9 1.4 maximum_select_fusion
  198.2 1.2 copy.48
  199.5 1.7 reshape.308
  201.2 9.3 %all-to-all-start = ((f32[128,1,256]{2,1,0:T(1,128)}), f32[128,1,256]{2,1,0:T(1,128)S(1)}, u32[]{:S(2)}, u32[]{:S(2)}) async-start(f32[128,1,256]{2,1,0:T(1,128)} %reshape.308), calls=%async_computation | async-start | bytes 262144 | tf_op jit(solution)/shard_map/all_to_all | solution.py:130
  210.5 12.2 %all-to-all-done = f32[128,1,256]{2,1,0:T(1,128)S(1)} async-done(((f32[128,1,256]{2,1,0:T(1,128)}), f32[128,1,256]{2,1,0:T(1,128)S(1)}, u32[]{:S(2)}, u32[]{:S(2)}) %all-to-all-start) | async-done | bytes 131104 | tf_op jit(solution)/shard_map/all_to_all | solution.py:130
  222.7 0.5 broadcast.282
  223.2 1.0 reduce.1
  224.1 2.5 reshape.309
  226.6 0.1 broadcast_in_dim.48
  226.8 33.1 %scatter_fusion = f32[8,8,512]{1,0,2:T(8,128)S(1)} fusion(f32[8,8,512]{1,0,2:T(8,128)S(1)} %broadcast_in_dim.48, s32[512]{0:T(512)S(1)} %compare_select_fusion, f32[512,8,8]{2,1,0:T(8,128)} %bitcast.77), kind=kCustom, calls=%fused_computation | custom fusion | bytes 395264 | tf_op jit(solution)/shard_map/scatter | solution.py:135
  259.9 1.3 copy.45
  (42 shorter events, 0.4 us)
Async XLA Ops:
  7.4 138.0 %copy-start = (bf16[768,768]{1,0:T(8,128)(2,1)S(1)}, bf16[768,768]{1,0:T(8,128)(2,1)}, u32[]{:S(2)}) copy-start(bf16[768,768]{1,0:T(8,128)(2,1)} %param.26) | copy-start | bytes 3538948
  7.4 4.7 %copy-start.1 = (bf16[1,256,768]{2,1,0:T(8,128)(2,1)S(1)}, bf16[1,256,768]{2,1,0:T(8,128)(2,1)}, u32[]{:S(2)}) copy-start(bf16[1,256,768]{2,1,0:T(8,128)(2,1)} %param.15) | copy-start | bytes 1179652
  7.4 4.7 %copy-start.4 = (f32[768]{0:T(1024)S(1)}, f32[768]{0:T(1024)}, u32[]{:S(2)}) copy-start(f32[768]{0:T(1024)} %param.19) | copy-start | bytes 9220
  7.4 69.0 %all-reduce.3.cloned.1.call-start = ((), (), s32[]{:S(2)}) async-start(), calls=%async_computation.1 | async-start | bytes 1572864 | tf_op jit(solution)/shard_map/psum | solution.py:99
  13.2 3.1 %copy-start.3 = (bf16[192,768]{1,0:T(8,128)(2,1)S(1)}, bf16[192,768]{1,0:T(8,128)(2,1)}, u32[]{:S(2)}) copy-start(bf16[192,768]{1,0:T(8,128)(2,1)} %param.21) | copy-start | bytes 884740
  16.2 63.0 %copy-start.5 = (f32[768]{0:T(1024)S(1)}, f32[768]{0:T(1024)}, u32[]{:S(2)}) copy-start(f32[768]{0:T(1024)} %param.22) | copy-start | bytes 9220
  17.5 126.3 %all-reduce.5.cloned.1.call-start = ((), (), s32[]{:S(2)}) async-start(), calls=%async_computation.2 | async-start | bytes 1572864 | tf_op jit(solution)/shard_map/psum | solution.py:105
  76.4 2.8 %copy-start.2 = (f32[256,768]{1,0:T(8,128)S(1)}, f32[256,768]{1,0:T(8,128)}, u32[]{:S(2)}) copy-start(f32[256,768]{1,0:T(8,128)} %all-reduce.3.cloned.1.call-done) | copy-start | bytes 2359300
  77.7 3.0 %copy-start.8 = (bf16[288,768]{1,0:T(8,128)(2,1)S(1)}, bf16[288,768]{1,0:T(8,128)(2,1)}, u32[]{:S(2)}) copy-start(bf16[288,768]{1,0:T(8,128)(2,1)} %param.24) | copy-start | bytes 1327108
  80.7 3.9 %copy-start.6 = (bf16[1,8,1,8]{3,1,2,0:T(8,128)(2,1)S(1)}, bf16[1,8,1,8]{3,1,2,0:T(8,128)(2,1)}, u32[]{:S(2)}) copy-start(bf16[1,8,1,8]{3,1,2,0:T(8,128)(2,1)} %param.29) | copy-start | bytes 388
  84.0 100.1 %all-gather.2.cloned.1.call-start = ((), (), s32[]{:S(2)}) async-start(), calls=%async_computation.3 | async-start | bytes 12681216 | tf_op jit(solution)/shard_map/all_gather | solution.py:113
  139.9 5.5 %copy-start.9 = (f32[768]{0:T(1024)S(1)}, f32[768]{0:T(1024)}, u32[]{:S(2)}) copy-start(f32[768]{0:T(1024)} %param.25) | copy-start | bytes 9220
  145.4 38.8 %copy-start.10 = (f32[768]{0:T(1024)S(1)}, f32[768]{0:T(1024)}, u32[]{:S(2)}) copy-start(f32[768]{0:T(1024)} %param.27) | copy-start | bytes 9220
  199.4 11.0 %copy-start.7 = (s32[512]{0:T(512)S(1)}, s32[512]{0:T(512)}, u32[]{:S(2)}) copy-start(s32[512]{0:T(512)} %param.18) | copy-start | bytes 6148
  201.2 21.5 %all-to-all-start = ((f32[128,1,256]{2,1,0:T(1,128)}), f32[128,1,256]{2,1,0:T(1,128)S(1)}, u32[]{:S(2)}, u32[]{:S(2)}) async-start(f32[128,1,256]{2,1,0:T(1,128)} %reshape.308), calls=%async_computation | async-start | bytes 262144 | tf_op jit(solution)/shard_map/all_to_all | solution.py:130
Sparse Core Ops, SparseCore 0:
  17.6 58.7 all-reduce.2
  84.1 56.7 all-reduce.4
Sparse Core Ops, SparseCore 1:
  87.8 96.3 all-gather.1
where the time goes:
time: 271 us; the launch traced here: 269 us
  waiting for transfers between devices  108 us (40%)
  blocking collectives  53.9 us (20%)
  local copies, waits for them, and re-layouts  47.1 us (17%)
  matrix products  22.3 us (8%)
  between operations  15.2 us (6%)
  other arithmetic  12.8 us (5%)
  starting transfers between devices  9.34 us (3%)
    psum x1, waiting for transfers between devices, on_device(): after_attn = tokens.astype(jnp.float32) + lax.psum(partial_attn, 'term')  58.9 us
    all_gather x1, blocking collectives, on_device(): rows_bias = lax.all_gather(decoder_bias, 'dp', axis=2, tiled=True)  53.9 us
    all_gather x1, waiting for transfers between devices, on_device(): rows_weight = lax.all_gather(decoder, 'dp', axis=2, tiled=True)  36.3 us
    scatter x1, local copies, waits for them, and re-layouts, on_device(): placed = jnp.zeros((groups, span, passages), jnp.float32).at[:, :, doc_id...  33.1 us
    all_to_all x1, waiting for transfers between devices, on_device(): lax.all_to_all(weighted, 'dp', split_axis=2, concat_axis=0, tiled=True)  12.2 us
    dot_general x1, matrix products, on_device(): lax.dot_general(headed, flat_rows, (((1,), (1,)), ((), ())), preferred_el...  10.7 us
    all_to_all x1, starting transfers between devices, on_device(): lax.all_to_all(weighted, 'dp', split_axis=2, concat_axis=0, tiled=True)  9.25 us
  transfers between devices with their start and end apart: 4, of which 3 were waited for; matrix products, arithmetic and copies ran while one was open for 3% of the time, Pallas kernels for 0%

commit v1 on v0

--- a/solution.py
+++ b/solution.py
@@ -96,7 +96,7 @@
     context = jnp.einsum("hqk,khd->qhd", probabilities, values, preferred_element_type=jnp.float32)
     context = context.astype(jnp.bfloat16).reshape(length, head_width)
     partial_attn = jnp.dot(context, attn_out, preferred_element_type=jnp.float32)
-    after_attn = tokens.astype(jnp.float32) + lax.psum(partial_attn, "term")
+    after_attn = tokens.astype(jnp.float32) + jnp.sum(lax.all_gather(partial_attn, "term"), axis=0)
     mixed_in = layer_norm(after_attn, mlp_gain).astype(jnp.bfloat16)
     inner_up = jnp.dot(mixed_in, ffn_in[0], preferred_element_type=jnp.float32)
     gate_part = jnp.dot(mixed_in, ffn_in[1], preferred_element_type=jnp.float32)

time: 271 us -> 259 us (0.956)
  waiting for transfers between devices: 108 us -> 98.5 us
    psum x1 -> x0, waiting for transfers between devices: 58.9 us -> none  [on_device(): after_attn = tokens.astype(jnp.float32) + lax.psum(partial_attn, 'term')]
    all_gather x0 -> x1, waiting for transfers between devices: none -> 50.5 us  [on_device(): lax.all_gather(partial_attn, 'term')]
  transfers between devices with their start and end apart: 4 -> 4, of which waited for: 3 -> 3; matrix products, arithmetic and copies ran while one was open for 3% -> 4% of each run, Pallas kernels for 0% -> 0%
where the time goes in v1:
time: 259 us; the launch traced here: 257 us
  waiting for transfers between devices  98.5 us (38%)
  blocking collectives  52.3 us (20%)
  local copies, waits for them, and re-layouts  47.7 us (18%)
  matrix products  21.3 us (8%)
  between operations  15.2 us (6%)
  other arithmetic  12.8 us (5%)
  starting transfers between devices  9.49 us (4%)
    all_gather x1, blocking collectives, on_device(): rows_bias = lax.all_gather(decoder_bias, 'dp', axis=2, tiled=True)  52.3 us
    all_gather x1, waiting for transfers between devices, on_device(): lax.all_gather(partial_attn, 'term')  50.5 us
    all_gather x1, waiting for transfers between devices, on_device(): rows_weight = lax.all_gather(decoder, 'dp', axis=2, tiled=True)  35.3 us
    scatter x1, local copies, waits for them, and re-layouts, on_device(): placed = jnp.zeros((groups, span, passages), jnp.float32).at[:, :, doc_id...  33.1 us
    all_to_all x1, waiting for transfers between devices, on_device(): lax.all_to_all(weighted, 'dp', split_axis=2, concat_axis=0, tiled=True)  12.2 us
    dot_general x1, matrix products, on_device(): lax.dot_general(headed, flat_rows, (((1,), (1,)), ((), ())), preferred_el...  10.7 us
    all_to_all x1, starting transfers between devices, on_device(): lax.all_to_all(weighted, 'dp', split_axis=2, concat_axis=0, tiled=True)  9.4 us
  transfers between devices with their start and end apart: 4, of which 3 were waited for; matrix products, arithmetic and copies ran while one was open for 4% of the time, Pallas kernels for 0%

profile of v1, /device:TPU:1, one launch (start us, length us, event | category | flops | bytes accessed | tf_op | source)
XLA Modules:
  0.0 257.1 jit_solution(12659715370079522254)
XLA Ops:
  7.4 0.8 constant_dynamic-slice_fusion
  8.5 1.1 convert_reduce_fusion
  9.6 1.2 fusion.9
  10.9 1.2 fusion.187
  12.1 0.2 fusion.35
  12.3 0.3 fusion.189
  12.6 0.3 fusion.190
  12.9 0.2 multiply_cosine_fusion
  13.2 1.2 fusion.3
  14.4 1.8 convolution_convert_fusion
  16.2 1.2 fusion.191
  17.5 50.5 %all-gather.6.cloned.1.call-done = f32[1024,768]{1,0:T(8,128)} async-done(((f32[256,768]{1,0:T(8,128)}), f32[1024,768]{1,0:T(8,128)}) %all-gather.6.cloned.1.call-update) | async-done | bytes 3145744 | tf_op jit(solution)/shard_map/all_gather | solution.py:99
  68.0 2.2 reduce_sum.105
  70.2 0.2 fusion.45
  70.3 0.2 multiply_reduce_fusion.2
  70.6 0.3 copy-done.5
  70.8 0.2 fusion.34
  71.0 0.3 copy-done.3
  71.3 0.3 fusion.28
  71.7 3.3 %fusion.5 = f32[256,768]{1,0:T(8,128)} fusion(bf16[288,768]{1,0:T(8,128)(2,1)S(1)} %copy-done.8, bf16[256,768]{1,0:T(8,128)(2,1)S(1)} %fusion.34, bf16[2,768,288]{1,2,0:T(8,128)(2,1)} %param.23, f32[256,288]{0,1:T(8,128)S(1)} %fusion.28), kind=kOutput, calls=%fused_computation.20 | convolution fusion | flops 231358464 | bytes 2359296 | tf_op jit(solution)/shard_map/dot_general | solution.py:104
  75.0 0.5 all-gather.4.cloned.1.call-update
  75.5 52.3 %all_gather.15 = bf16[1,8,128,8]{3,1,0,2:T(8,128)(2,1)S(1)} all-gather(bf16[1,8,1,8]{3,1,0,2:T(8,128)(2,1)S(1)} %bitcast.92), channel_id=1, replica_groups=mesh['dp'=128,'term'=4] {'dp'}, dimensions={2}, use_global_device_ids=true | all-gather | bytes 16512 | tf_op jit(solution)/shard_map/all_gather | solution.py:114
  127.8 0.2 copy.42
  128.0 0.1 copy.43
  128.1 0.3 reshape.340
  128.4 0.7 constant_dynamic-slice_fusion.1
  129.1 2.6 %compare_reduce_fusion = pred[4,8192]{1,0:T(4,128)(4,1)S(1)} fusion(s32[8192]{0:T(1024)S(1)} %add_select_fusion, s32[4,128]{1,0:T(4,128)S(1)} %constant_dynamic-slice_fusion.1), kind=kLoop, calls=%fused_computation.1 | loop fusion | flops 8355840 | bytes 67584 | tf_op jit(solution)/shard_map/reduce_or | solution.py:126
  131.8 1.3 reduce_or.12
  133.1 1.5 fusion.185
  134.6 0.2 multiply_reduce_fusion.1
  134.8 2.2 fusion.188
  137.0 0.2 multiply_reduce_fusion
  137.2 35.3 %all-gather.4.cloned.1.call-done = bf16[1,8,128,8,768]{4,3,2,1,0:T(8,128)(2,1)} async-done(((bf16[1,8,1,8,768]{4,3,2,1,0:T(8,128)(2,1)}), bf16[1,8,128,8,768]{4,3,2,1,0:T(8,128)(2,1)}) %all-gather.4.cloned.1.call-update) | async-done | bytes 12582928 | tf_op jit(solution)/shard_map/all_gather | solution.py:113
  172.5 10.7 %select_reduce_fusion.3 = (f32[8192]{0:T(1024)S(1)}, f32[8192]{0:T(1024)S(1)}, f32[8192]{0:T(1024)S(1)}, f32[8192]{0:T(1024)S(1)}) fusion(pred[256]{0:T(512)(128)(4,1)S(1)} %get-tuple-element.25, pred[256]{0:T(512)(128)(4,1)S(1)} %get-tuple-element.23, pred[256]{0:T(512)(128)(4,1)S(1)} %get-tuple-element.24, pred[256]{0:T(512)(128)(4,1)S(1)} %get-tuple-element.22, ...), kind=kOutput, calls=%fused_computation.8 | convolution fusion | flops 3242950656 | bytes 13539328 | tf_op jit(solution)/shard_map/dot_general | solution.py:117
  183.2 0.3 stack.15
  183.5 0.3 stack.16
  183.8 0.3 stack.17
  184.1 1.1 stack.18
  185.2 1.4 maximum_select_fusion
  186.6 1.2 copy.48
  187.8 1.7 reshape.352
  189.6 9.4 %all-to-all-start = ((f32[128,1,256]{2,1,0:T(1,128)}), f32[128,1,256]{2,1,0:T(1,128)S(1)}, u32[]{:S(2)}, u32[]{:S(2)}) async-start(f32[128,1,256]{2,1,0:T(1,128)} %reshape.352), calls=%async_computation | async-start | bytes 262144 | tf_op jit(solution)/shard_map/all_to_all | solution.py:130
  199.0 12.2 %all-to-all-done = f32[128,1,256]{2,1,0:T(1,128)S(1)} async-done(((f32[128,1,256]{2,1,0:T(1,128)}), f32[128,1,256]{2,1,0:T(1,128)S(1)}, u32[]{:S(2)}, u32[]{:S(2)}) %all-to-all-start) | async-done | bytes 131104 | tf_op jit(solution)/shard_map/all_to_all | solution.py:130
  211.2 0.5 broadcast.303
  211.7 1.0 reduce.1
  212.6 2.5 reshape.353
  215.3 33.1 %scatter_fusion = f32[8,8,512]{1,0,2:T(8,128)S(1)} fusion(f32[8,8,512]{1,0,2:T(8,128)S(1)} %broadcast_in_dim.48, s32[512]{0:T(512)S(1)} %compare_select_fusion, f32[512,8,8]{2,1,0:T(8,128)} %bitcast.82), kind=kCustom, calls=%fused_computation | custom fusion | bytes 395264 | tf_op jit(solution)/shard_map/scatter | solution.py:135
  248.4 1.3 copy.45
  (43 shorter events, 0.7 us)
Async XLA Ops:
  7.4 127.4 %copy-start = (bf16[768,768]{1,0:T(8,128)(2,1)S(1)}, bf16[768,768]{1,0:T(8,128)(2,1)}, u32[]{:S(2)}) copy-start(bf16[768,768]{1,0:T(8,128)(2,1)} %param.26) | copy-start | bytes 3538948
  7.4 4.7 %copy-start.1 = (bf16[1,256,768]{2,1,0:T(8,128)(2,1)S(1)}, bf16[1,256,768]{2,1,0:T(8,128)(2,1)}, u32[]{:S(2)}) copy-start(bf16[1,256,768]{2,1,0:T(8,128)(2,1)} %param.15) | copy-start | bytes 1179652
  7.4 4.7 %copy-start.4 = (f32[768]{0:T(1024)S(1)}, f32[768]{0:T(1024)}, u32[]{:S(2)}) copy-start(f32[768]{0:T(1024)} %param.19) | copy-start | bytes 9220
  7.4 60.6 %all-gather.6.cloned.1.call-start = ((), (), s32[]{:S(2)}) async-start(), calls=%async_computation.3 | async-start | bytes 3932160 | tf_op jit(solution)/shard_map/all_gather | solution.py:99
  13.2 3.1 %copy-start.2 = (bf16[192,768]{1,0:T(8,128)(2,1)S(1)}, bf16[192,768]{1,0:T(8,128)(2,1)}, u32[]{:S(2)}) copy-start(bf16[192,768]{1,0:T(8,128)(2,1)} %param.21) | copy-start | bytes 884740
  17.4 115.6 %all-reduce.2.cloned.1.call-start = ((), (), s32[]{:S(2)}) async-start(), calls=%async_computation.1 | async-start | bytes 1572864 | tf_op jit(solution)/shard_map/psum | solution.py:105
  70.1 0.7 copy-start.5
  70.1 1.2 copy-start.3
  70.3 1.3 copy-start.8
  71.6 3.9 %copy-start.6 = (bf16[1,8,1,8]{3,1,2,0:T(8,128)(2,1)S(1)}, bf16[1,8,1,8]{3,1,2,0:T(8,128)(2,1)}, u32[]{:S(2)}) copy-start(bf16[1,8,1,8]{3,1,2,0:T(8,128)(2,1)} %param.29) | copy-start | bytes 388
  74.9 97.6 %all-gather.4.cloned.1.call-start = ((), (), s32[]{:S(2)}) async-start(), calls=%async_computation.2 | async-start | bytes 12681216 | tf_op jit(solution)/shard_map/all_gather | solution.py:113
  129.1 5.7 %copy-start.9 = (f32[768]{0:T(1024)S(1)}, f32[768]{0:T(1024)}, u32[]{:S(2)}) copy-start(f32[768]{0:T(1024)} %param.25) | copy-start | bytes 9220
  134.8 37.7 %copy-start.10 = (f32[768]{0:T(1024)S(1)}, f32[768]{0:T(1024)}, u32[]{:S(2)}) copy-start(f32[768]{0:T(1024)} %param.27) | copy-start | bytes 9220
  187.8 11.1 %copy-start.7 = (s32[512]{0:T(512)S(1)}, s32[512]{0:T(512)}, u32[]{:S(2)}) copy-start(s32[512]{0:T(512)} %param.18) | copy-start | bytes 6148
  189.6 21.6 %all-to-all-start = ((f32[128,1,256]{2,1,0:T(1,128)}), f32[128,1,256]{2,1,0:T(1,128)S(1)}, u32[]{:S(2)}, u32[]{:S(2)}) async-start(f32[128,1,256]{2,1,0:T(1,128)} %reshape.352), calls=%async_computation | async-start | bytes 262144 | tf_op jit(solution)/shard_map/all_to_all | solution.py:130
Sparse Core Ops, SparseCore 0:
  17.6 50.3 all-gather.5
  75.1 54.0 all-reduce.1
Sparse Core Ops, SparseCore 1:
  78.7 93.8 all-gather.3
